TPU v7x, 256 devices: a whole 4x4x8 slice. The times are simulated.
256 devices in a mesh: prompt: 4 (over x), vocab: 64 (over z, y, core).
Axes of the slice: x: 4, y: 4, z: 8, core: 2. Of those that a mesh axis runs over, the one named last changes fastest.
Arguments:
- hidden: bfloat16 [512, 8192], P('prompt')
- head: bfloat16 [8192, 65536], P('prompt', 'vocab')
- gain: float32 [8192], replicated, may hold values from 0.25 to 1.75
- refusal_ids: int32 [512, 16], P('prompt'), may hold values from 0 to 65535, as said below
- refusal_count: int32 [512], P('prompt'), may hold values from 1 to 16
- loss_scale: float32 [512], P('prompt'), may hold values from 8 to 32
Outputs:
- grad_hidden: float32 [512, 8192], P('prompt', 'vocab')
- log_refusal: float32 [512], P('prompt')
Inputs may be any that keep to these rules, and one draw needn't show every extreme that they name: `refusal_ids`: the first refusal_count entries of a prompt's list are distinct ids below 65536; later entries are ignored.
All inputs are finite; a program needn't handle non-finite values.
Results may differ from a plain program's by a relative error of at most 0.0027.
The roundings to bfloat16 on the way count: a program that leaves them out, or rounds other values in their place, can miss the bound.
Values may be sent and summed in bfloat16 or wider, within the bound.
A program may use at most 128 MiB of HBM per device.

v0:
```python
import jax
import jax.numpy as jnp
from jax import lax
from jax.sharding import PartitionSpec as P

epsilon = 1e-05
lowest = -1e30


def shards(hidden, head, gain, refusal_ids, refusal_count, loss_scale):
    row_count, model_width = hidden.shape
    vocab_local = head.shape[1]
    list_length = refusal_ids.shape[1]
    hidden_f = hidden.astype(jnp.float32)
    inverse_rms = lax.rsqrt(jnp.mean(hidden_f * hidden_f, axis=1, keepdims=True) + epsilon)
    normed = (hidden_f * inverse_rms * gain).astype(jnp.bfloat16)
    logits = jnp.dot(
        normed,
        lax.all_gather(head, "prompt", axis=0, tiled=True),
        preferred_element_type=jnp.float32,
    )
    vocab_start = lax.axis_index("vocab") * vocab_local
    shifted_ids = refusal_ids - vocab_start
    in_list = jnp.arange(list_length)[None, :] < refusal_count[:, None]
    is_local = in_list & (shifted_ids >= 0) & (shifted_ids < vocab_local)
    safe_ids = jnp.clip(shifted_ids, 0, vocab_local - 1)
    picked = jnp.take_along_axis(logits, safe_ids, axis=1)
    peak_all = jnp.max(logits, axis=1)
    peak_ref = jnp.max(jnp.where(is_local, picked, lowest), axis=1)
    peak_all, peak_ref = lax.pmax((peak_all, peak_ref), "vocab")
    sum_all = jnp.sum(jnp.exp(logits - peak_all[:, None]), axis=1)
    sum_ref = jnp.sum(jnp.exp(jnp.where(is_local, picked - peak_ref[:, None], lowest)), axis=1)
    sum_all, sum_ref = lax.psum((sum_all, sum_ref), "vocab")
    lse_all = peak_all + jnp.log(sum_all)
    lse_ref = peak_ref + jnp.log(sum_ref)
    log_refusal = lse_ref - lse_all
    member = jnp.any(
        (safe_ids[:, :, None] == jnp.arange(vocab_local)[None, None, :]) & is_local[:, :, None],
        axis=1,
    )
    grad_logits = loss_scale[:, None] * (
        jnp.exp(jnp.where(member, logits - lse_ref[:, None], lowest))
        - jnp.exp(logits - lse_all[:, None])
    )
    grad_b = grad_logits.astype(jnp.bfloat16)
    slice_width = model_width // lax.axis_size("vocab")
    col_start = lax.axis_index("vocab") * slice_width
    grad_full = lax.dot_general(
        grad_b,
        lax.all_gather(head, "prompt", axis=0, tiled=True),
        (((1,), (1,)), ((), ())),
        preferred_element_type=jnp.float32,
    )
    grad_cols = lax.psum_scatter(grad_full, "vocab", scatter_dimension=1, tiled=True)
    normed_cols = lax.dynamic_slice_in_dim(normed, col_start, slice_width, 1).astype(jnp.float32)
    row_term = lax.psum(jnp.sum(grad_cols * normed_cols, axis=1), "vocab")
    hidden_cols = lax.dynamic_slice_in_dim(hidden_f, col_start, slice_width, 1)
    gain_cols = lax.dynamic_slice_in_dim(gain, col_start, slice_width, 0)
    grad_hidden = (
        inverse_rms * gain_cols * grad_cols
        - hidden_cols * (inverse_rms * inverse_rms / model_width) * row_term[:, None]
    )
    return (grad_hidden, log_refusal)


def solution(mesh):
    return jax.shard_map(
        shards,
        mesh=mesh,
        in_specs=(
            P("prompt", None),
            P("prompt", "vocab"),
            P(),
            P("prompt", None),
            P("prompt"),
            P("prompt"),
        ),
        out_specs=(P("prompt", "vocab"), P("prompt")),
        check_vma=False,
    )
```

profile of v0, /device:TPU:1, one launch (start us, length us, event | category | flops | bytes accessed | tf_op | source)
XLA Modules:
  0.0 739.2 jit_solution(6245504685200072266)
XLA Ops:
  7.2 0.0 copy-start.2
  7.2 0.0 copy-start
  7.2 0.0 copy-start.1
  7.2 0.0 all-gather.2.cloned.1.call-start
  7.2 0.7 all-gather.2.cloned.1.call-update
  7.9 0.0 reduce-scatter.2.cloned.1.call-start
  8.0 0.0 copy-done.2
  8.0 0.1 copy.11
  8.1 0.1 reshape.39
  8.2 0.6 copy-done
  8.8 0.5 multiply_reduce_fusion
  9.3 0.0 copy-done.1
  9.3 1.9 multiply_convert_fusion
  11.2 159.1 %all-gather.2.cloned.1.call-done = bf16[8192,1024]{1,0:T(8,128)(2,1)} async-done(((bf16[2048,1024]{1,0:T(8,128)(2,1)}), bf16[8192,1024]{1,0:T(8,128)(2,1)}) %all-gather.2.cloned.1.call-update) | async-done | bytes 16777232 | tf_op jit(solution)/shard_map/all_gather | solution.py:19
  170.3 8.8 %fusion.12 = (f32[128]{0:T(128)S(1)}, f32[128,1024]{1,0:T(8,128)S(1)}) fusion(bf16[128,8192]{1,0:T(8,128)(2,1)} %multiply_convert_fusion, bf16[8192,1024]{1,0:T(8,128)(2,1)} %all-gather.2.cloned.1.call-done), kind=kOutput, calls=%fused_computation.30 | convolution fusion | flops 2147614720 | bytes 19399168 | tf_op jit(solution)/shard_map/dot_general | solution.py:17
  179.1 0.0 copy-start.4
  179.1 0.0 copy-start.3
  179.2 16.6 %gather_fusion = f32[2048]{0:T(1024)S(1)} fusion(f32[128,1024]{1,0:T(8,128)S(1)} %get-tuple-element.16, s32[2048]{0:T(1024)S(1)} %reshape.39), kind=kCustom, calls=%fused_computation | custom fusion | bytes 32768 | tf_op jit(solution)/shard_map/jit(take_along_axis)/gather | solution.py:27
  195.8 0.1 reshape.42
  195.9 0.0 copy-done.4
  195.9 0.2 select_reduce_fusion
  196.1 2.4 fusion.1
  198.5 124.6 %all-reduce.1 = (f32[128]{0:T(128)S(1)}, f32[128]{0:T(128)S(1)}) all-reduce(f32[128]{0:T(128)S(1)} %get-tuple-element.15, f32[128]{0:T(128)S(1)} %get-tuple-element.9), channel_id=1, replica_groups=mesh['prompt'=4,'vocab'=64] {'vocab'}, use_global_device_ids=true, to_apply=%region_7.8 | all-reduce | flops 256 | bytes 2048 | tf_op jit(solution)/shard_map/pmax | solution.py:30
  323.1 0.2 exponential_reduce_fusion.1
  323.3 0.2 exponential_reduce_fusion
  323.5 128.4 %all-reduce = (f32[128]{0:T(128)S(1)}, f32[128]{0:T(128)S(1)}) all-reduce(f32[128]{0:T(128)S(1)} %exponential_reduce_fusion, f32[128]{0:T(128)S(1)} %exponential_reduce_fusion.1), channel_id=1, replica_groups=mesh['prompt'=4,'vocab'=64] {'vocab'}, use_global_device_ids=true, to_apply=%region_9.10 | all-reduce | flops 256 | bytes 2048 | tf_op jit(solution)/shard_map/psum | solution.py:33
  452.0 0.5 fusion.10
  452.5 0.0 copy-done.3
  452.5 13.4 %fusion.2 = f32[128,8192]{1,0:T(8,128)} fusion(bf16[8192,1024]{1,0:T(8,128)(2,1)} %all-gather.2.cloned.1.call-done, f32[128,1024]{1,0:T(8,128)S(1)} %get-tuple-element.16, pred[128,1024]{1,0:T(8,128)(4,1)S(1)} %fusion.1, f32[128]{0:T(128)S(1)} %get-tuple-element.8, f32[128]{0:T(128)S(1)} %get-tuple-element.7, f32[128]{0:T(128)S(1)} %copy-done.3), kind=kOutput, calls=%fused_computation.8 | convolution fusion | flops 2148270080 | bytes 21628416 | tf_op jit(solution)/shard_map/dot_general | solution.py:48
  466.0 0.0 reduce-scatter.2.cloned.1.call-update
  466.0 2.3 convert_element_type.12
  468.3 0.1 dynamic_slice.9
  468.4 132.1 %reduce-scatter.2.cloned.1.call-done = f32[128,128]{1,0:T(8,128)} async-done(((f32[128,8192]{1,0:T(8,128)}), f32[128,128]{1,0:T(8,128)}) %reduce-scatter.2.cloned.1.call-update) | async-done | bytes 65552 | tf_op jit(solution)/shard_map/reduce_scatter | solution.py:54
  600.5 0.9 multiply_reduce_fusion.1
  601.5 129.2 %psum.23 = f32[128]{0:T(128)S(1)} all-reduce(f32[128]{0:T(128)S(1)} %multiply_reduce_fusion.1), channel_id=1, replica_groups=mesh['prompt'=4,'vocab'=64] {'vocab'}, use_global_device_ids=true, to_apply=%region_12.13 | all-reduce | flops 128 | bytes 1024 | tf_op jit(solution)/shard_map/psum | solution.py:56
  730.7 1.6 multiply_subtract_fusion
  (2 shorter events, 0.0 us)
Async XLA Ops:
  7.2 0.8 copy-start.2
  7.2 1.6 copy-start
  7.2 2.1 copy-start.1
  7.2 163.1 %all-gather.2.cloned.1.call-start = ((), (), s32[]{:S(2)}) async-start(), calls=%async_computation.1 | async-start | bytes 20971520 | tf_op jit(solution)/shard_map/all_gather | solution.py:19
  7.9 592.6 %reduce-scatter.2.cloned.1.call-start = ((), (), s32[]{:S(2)}) async-start(), calls=%async_computation.2 | async-start | bytes 4259840 | tf_op jit(solution)/shard_map/reduce_scatter | solution.py:54
  179.1 16.8 %copy-start.4 = (s32[128]{0:T(128)S(1)}, s32[128]{0:T(128)}, u32[]{:S(2)}) copy-start(s32[128]{0:T(128)} %param.10) | copy-start | bytes 1540
  179.1 273.4 %copy-start.3 = (f32[128]{0:T(128)S(1)}, f32[128]{0:T(128)}, u32[]{:S(2)}) copy-start(f32[128]{0:T(128)} %param.11) | copy-start | bytes 1540
Sparse Core Ops, SparseCore 0:
  9.8 160.4 all-gather.1
  466.1 134.3 reduce-scatter.1
where the time goes:
time: 739 us
  blocking collectives  382 us (52%)
  waiting for transfers between devices  292 us (40%)
  matrix products  22.3 us (3%)
  local copies, waits for them, and re-layouts  17.6 us (2%)
  between operations  14.2 us (2%)
  other arithmetic  10.9 us (1%)
    all_gather x1, waiting for transfers between devices, shards(): lax.all_gather(head, 'prompt', axis=0, tiled=True)  159 us
    reduce_scatter x1, waiting for transfers between devices, shards(): lax.psum_scatter(grad_full, 'vocab', scatter_dimension=1, tiled=True)  132 us
    psum x1, blocking collectives, shards(): row_term = lax.psum(jnp.sum(grad_cols * normed_cols, axis=1), 'vocab')  129 us
    psum x1, blocking collectives, shards(): sum_all, sum_ref = lax.psum((sum_all, sum_ref), 'vocab')  128 us
    pmax x1, blocking collectives, shards(): peak_all, peak_ref = lax.pmax((peak_all, peak_ref), 'vocab')  125 us
    gather x3, local copies, waits for them, and re-layouts, shards(): picked = jnp.take_along_axis(logits, safe_ids, axis=1)  16.8 us
  transfers between devices with their start and end apart: 2, of which 2 were waited for; matrix products, arithmetic and copies ran while one was open for 1% of the time, Pallas kernels for 0%

commit v1 on v0

--- a/solution.py
+++ b/solution.py
@@ -16,7 +16,15 @@
     normed = (hidden_f * inverse_rms * gain).astype(jnp.bfloat16)
     logits = jnp.dot(
         normed,
-        lax.all_gather(head, "prompt", axis=0, tiled=True),
+        jnp.concatenate(
+            lax.all_to_all(
+                jnp.stack([head for _ in range(lax.axis_size("prompt"))], 0),
+                split_axis=0,
+                concat_axis=0,
+                axis_name="prompt",
+            ),
+            0,
+        ),
         preferred_element_type=jnp.float32,
     )
     vocab_start = lax.axis_index("vocab") * vocab_local

time: 739 us -> 910 us (1.23)
  waiting for transfers between devices: 292 us -> 444 us
    all_to_all x0 -> x1, waiting for transfers between devices: none -> 314 us  [shards(): lax.all_to_all(jnp.stack([head for _ in range(lax.axis_size('prompt'))],...]
    all_gather x1, waiting for transfers between devices: 159 us -> 0.02 us  [shards(): lax.all_gather(head, 'prompt', axis=0, tiled=True)]
  transfers between devices with their start and end apart: 2 -> 3, of which waited for: 2 -> 2; matrix products, arithmetic and copies ran while one was open for 1% -> 5% of each run, Pallas kernels for 0% -> 0%
where the time goes in v1:
time: 910 us
  waiting for transfers between devices  444 us (49%)
  blocking collectives  387 us (43%)
  local copies, waits for them, and re-layouts  24.5 us (3%)
  matrix products  22.3 us (2%)
  between operations  14.2 us (2%)
  other arithmetic  10.9 us (1%)
    all_to_all x1, waiting for transfers between devices, shards(): lax.all_to_all(jnp.stack([head for _ in range(lax.axis_size('prompt'))],...  314 us
    pmax x1, blocking collectives, shards(): peak_all, peak_ref = lax.pmax((peak_all, peak_ref), 'vocab')  130 us
    psum x1, blocking collectives, shards(): row_term = lax.psum(jnp.sum(grad_cols * normed_cols, axis=1), 'vocab')  129 us
    reduce_scatter x1, waiting for transfers between devices, shards(): lax.psum_scatter(grad_full, 'vocab', scatter_dimension=1, tiled=True)  129 us
    psum x1, blocking collectives, shards(): sum_all, sum_ref = lax.psum((sum_all, sum_ref), 'vocab')  128 us
  transfers between devices with their start and end apart: 3, of which 2 were waited for; matrix products, arithmetic and copies ran while one was open for 5% of the time, Pallas kernels for 0%

profile of v1, /device:TPU:1, one launch (start us, length us, event | category | flops | bytes accessed | tf_op | source)
XLA Modules:
  0.0 910.0 jit_solution(3506879918497108284)
XLA Ops:
  7.2 0.0 all-gather.2.cloned.1.call-start
  7.2 0.7 all-gather.2.cloned.1.call-update
  7.9 7.5 stack.2
  15.4 0.0 copy-start.2
  15.4 0.0 copy-start
  15.4 0.0 copy-start.1
  15.4 7.1 all-to-all-start
  22.5 0.0 reduce-scatter.2.cloned.1.call-start
  22.5 0.0 copy-done.2
  22.5 0.1 copy.11
  22.7 0.1 reshape.45
  22.8 0.0 copy-done
  22.8 0.5 multiply_reduce_fusion
  23.3 0.0 copy-done.1
  23.3 1.9 multiply_convert_fusion
  25.2 313.9 %all-to-all-done = bf16[4,2048,1024]{2,1,0:T(8,128)(2,1)} async-done(((bf16[4,2048,1024]{2,1,0:T(8,128)(2,1)}), bf16[4,2048,1024]{2,1,0:T(8,128)(2,1)}, u32[]{:S(2)}, u32[]{:S(2)}) %all-to-all-start) | async-done | bytes 16777248 | tf_op jit(solution)/shard_map/all_to_all | solution.py:20
  339.1 8.8 fusion.12
  347.9 0.0 copy-start.4
  347.9 0.0 copy-start.3
  348.0 16.6 %gather_fusion = f32[2048]{0:T(1024)S(1)} fusion(f32[128,1024]{1,0:T(8,128)S(1)} %get-tuple-element.16, s32[2048]{0:T(1024)S(1)} %reshape.45), kind=kCustom, calls=%fused_computation | custom fusion | bytes 32768 | tf_op jit(solution)/shard_map/jit(take_along_axis)/gather | solution.py:35
  364.6 0.1 reshape.48
  364.7 0.0 copy-done.4
  364.7 0.2 select_reduce_fusion
  364.9 130.4 %all-reduce.1 = (f32[128]{0:T(128)S(1)}, f32[128]{0:T(128)S(1)}) all-reduce(f32[128]{0:T(128)S(1)} %get-tuple-element.15, f32[128]{0:T(128)S(1)} %get-tuple-element.9), channel_id=1, replica_groups=mesh['prompt'=4,'vocab'=64] {'vocab'}, use_global_device_ids=true, to_apply=%region_7.8 | all-reduce | flops 256 | bytes 2048 | tf_op jit(solution)/shard_map/pmax | solution.py:38
  495.3 0.2 exponential_reduce_fusion.1
  495.5 0.2 exponential_reduce_fusion
  495.7 127.5 %all-reduce = (f32[128]{0:T(128)S(1)}, f32[128]{0:T(128)S(1)}) all-reduce(f32[128]{0:T(128)S(1)} %exponential_reduce_fusion, f32[128]{0:T(128)S(1)} %exponential_reduce_fusion.1), channel_id=1, replica_groups=mesh['prompt'=4,'vocab'=64] {'vocab'}, use_global_device_ids=true, to_apply=%region_9.10 | all-reduce | flops 256 | bytes 2048 | tf_op jit(solution)/shard_map/psum | solution.py:41
  623.3 0.5 fusion.10
  623.8 2.4 fusion.1
  626.2 0.0 all-gather.2.cloned.1.call-done
  626.2 0.0 copy-done.3
  626.2 13.5 %fusion.2 = f32[128,8192]{1,0:T(8,128)} fusion(bf16[8192,1024]{1,0:T(8,128)(2,1)} %all-gather.2.cloned.1.call-done, f32[128,1024]{1,0:T(8,128)S(1)} %get-tuple-element.16, pred[128,1024]{1,0:T(8,128)(4,1)S(1)} %fusion.1, f32[128]{0:T(128)S(1)} %get-tuple-element.8, f32[128]{0:T(128)S(1)} %get-tuple-element.7, f32[128]{0:T(128)S(1)} %copy-done.3), kind=kOutput, calls=%fused_computation.8 | convolution fusion | flops 2148270080 | bytes 21628416 | tf_op jit(solution)/shard_map/dot_general | solution.py:56
  639.7 0.0 reduce-scatter.2.cloned.1.call-update
  639.7 2.4 convert_element_type.12
  642.1 0.1 dynamic_slice.9
  642.1 129.2 %reduce-scatter.2.cloned.1.call-done = f32[128,128]{1,0:T(8,128)} async-done(((f32[128,8192]{1,0:T(8,128)}), f32[128,128]{1,0:T(8,128)}) %reduce-scatter.2.cloned.1.call-update) | async-done | bytes 65552 | tf_op jit(solution)/shard_map/reduce_scatter | solution.py:62
  771.4 0.9 multiply_reduce_fusion.1
  772.3 129.2 %psum.23 = f32[128]{0:T(128)S(1)} all-reduce(f32[128]{0:T(128)S(1)} %multiply_reduce_fusion.1), channel_id=1, replica_groups=mesh['prompt'=4,'vocab'=64] {'vocab'}, use_global_device_ids=true, to_apply=%region_12.13 | all-reduce | flops 128 | bytes 1024 | tf_op jit(solution)/shard_map/psum | solution.py:64
  901.6 1.6 multiply_subtract_fusion
  (2 shorter events, 0.0 us)
Async XLA Ops:
  7.2 619.1 %all-gather.2.cloned.1.call-start = ((), (), s32[]{:S(2)}) async-start(), calls=%async_computation.2 | async-start | bytes 20971520 | tf_op jit(solution)/shard_map/all_gather | solution.py:58
  15.4 7.2 copy-start.2
  15.4 7.4 copy-start
  15.4 7.9 copy-start.1
  15.4 323.7 %all-to-all-start = ((bf16[4,2048,1024]{2,1,0:T(8,128)(2,1)}), bf16[4,2048,1024]{2,1,0:T(8,128)(2,1)}, u32[]{:S(2)}, u32[]{:S(2)}) async-start(bf16[4,2048,1024]{2,1,0:T(8,128)(2,1)} %stack.2), calls=%async_computation | async-start | bytes 33554432 | tf_op jit(solution)/shard_map/all_to_all | solution.py:20
  22.5 748.9 %reduce-scatter.2.cloned.1.call-start = ((), (), s32[]{:S(2)}) async-start(), calls=%async_computation.3 | async-start | bytes 4259840 | tf_op jit(solution)/shard_map/reduce_scatter | solution.py:62
  347.9 16.8 %copy-start.4 = (s32[128]{0:T(128)S(1)}, s32[128]{0:T(128)}, u32[]{:S(2)}) copy-start(s32[128]{0:T(128)} %param.10) | copy-start | bytes 1540
  347.9 278.3 %copy-start.3 = (f32[128]{0:T(128)S(1)}, f32[128]{0:T(128)}, u32[]{:S(2)}) copy-start(f32[128]{0:T(128)} %param.11) | copy-start | bytes 1540
Sparse Core Ops, SparseCore 0:
  9.8 295.6 all-gather.1
  639.8 131.4 reduce-scatter.1

commit v2 on v0

--- a/solution.py
+++ b/solution.py
@@ -53,7 +53,9 @@
     )
     grad_cols = lax.psum_scatter(grad_full, "vocab", scatter_dimension=1, tiled=True)
     normed_cols = lax.dynamic_slice_in_dim(normed, col_start, slice_width, 1).astype(jnp.float32)
-    row_term = lax.psum(jnp.sum(grad_cols * normed_cols, axis=1), "vocab")
+    own = jnp.sum(grad_cols * normed_cols, axis=1)
+    pieces = lax.all_gather(own, "vocab")
+    row_term = jnp.sum(pieces, axis=0)
     hidden_cols = lax.dynamic_slice_in_dim(hidden_f, col_start, slice_width, 1)
     gain_cols = lax.dynamic_slice_in_dim(gain, col_start, slice_width, 0)
     grad_hidden = (

time: 739 us -> 654 us (0.88)
  blocking collectives: 382 us -> 297 us
    psum x1 -> x0, blocking collectives: 129 us -> none  [shards(): row_term = lax.psum(jnp.sum(grad_cols * normed_cols, axis=1), 'vocab')]
    all_gather x0 -> x1, blocking collectives: none -> 43.7 us  [shards(): pieces = lax.all_gather(own, 'vocab')]
where the time goes in v2:
time: 654 us
  blocking collectives  297 us (45%)
  waiting for transfers between devices  292 us (45%)
  matrix products  22.3 us (3%)
  local copies, waits for them, and re-layouts  17.6 us (3%)
  between operations  14.2 us (2%)
  other arithmetic  11 us (2%)
    all_gather x1, waiting for transfers between devices, shards(): lax.all_gather(head, 'prompt', axis=0, tiled=True)  159 us
    reduce_scatter x1, waiting for transfers between devices, shards(): lax.psum_scatter(grad_full, 'vocab', scatter_dimension=1, tiled=True)  132 us
    psum x1, blocking collectives, shards(): sum_all, sum_ref = lax.psum((sum_all, sum_ref), 'vocab')  128 us
    pmax x1, blocking collectives, shards(): peak_all, peak_ref = lax.pmax((peak_all, peak_ref), 'vocab')  125 us
    all_gather x1, blocking collectives, shards(): pieces = lax.all_gather(own, 'vocab')  43.7 us
    gather x3, local copies, waits for them, and re-layouts, shards(): picked = jnp.take_along_axis(logits, safe_ids, axis=1)  16.8 us
    dot_general x1, matrix products, shards(): lax.dot_general(grad_b, lax.all_gather(head, 'prompt', axis=0, tiled=True...  13.4 us
  transfers between devices with their start and end apart: 2, of which 2 were waited for; matrix products, arithmetic and copies ran while one was open for 1% of the time, Pallas kernels for 0%

profile of v2, /device:TPU:1, one launch (start us, length us, event | category | flops | bytes accessed | tf_op | source)
XLA Modules:
  0.0 653.8 jit_solution(11738363051979935627)
XLA Ops:
  7.2 0.0 copy-start.2
  7.2 0.0 copy-start
  7.2 0.0 copy-start.1
  7.2 0.0 all-gather.4.cloned.1.call-start
  7.2 0.7 all-gather.4.cloned.1.call-update
  7.9 0.0 reduce-scatter.2.cloned.1.call-start
  8.0 0.0 copy-done.2
  8.0 0.1 copy.12
  8.1 0.1 reshape.39
  8.2 0.6 copy-done
  8.8 0.5 multiply_reduce_fusion
  9.3 0.0 copy-done.1
  9.3 1.9 multiply_convert_fusion
  11.2 159.1 %all-gather.4.cloned.1.call-done = bf16[8192,1024]{1,0:T(8,128)(2,1)} async-done(((bf16[2048,1024]{1,0:T(8,128)(2,1)}), bf16[8192,1024]{1,0:T(8,128)(2,1)}) %all-gather.4.cloned.1.call-update) | async-done | bytes 16777232 | tf_op jit(solution)/shard_map/all_gather | solution.py:19
  170.3 8.8 %fusion.12 = (f32[128]{0:T(128)S(1)}, f32[128,1024]{1,0:T(8,128)S(1)}) fusion(bf16[128,8192]{1,0:T(8,128)(2,1)} %multiply_convert_fusion, bf16[8192,1024]{1,0:T(8,128)(2,1)} %all-gather.4.cloned.1.call-done), kind=kOutput, calls=%fused_computation.30 | convolution fusion | flops 2147614720 | bytes 19399168 | tf_op jit(solution)/shard_map/dot_general | solution.py:17
  179.1 0.0 copy-start.4
  179.1 0.0 copy-start.3
  179.2 16.6 %gather_fusion = f32[2048]{0:T(1024)S(1)} fusion(f32[128,1024]{1,0:T(8,128)S(1)} %get-tuple-element.16, s32[2048]{0:T(1024)S(1)} %reshape.39), kind=kCustom, calls=%fused_computation | custom fusion | bytes 32768 | tf_op jit(solution)/shard_map/jit(take_along_axis)/gather | solution.py:27
  195.8 0.1 reshape.42
  195.9 0.0 copy-done.4
  195.9 0.2 select_reduce_fusion
  196.1 2.4 fusion.1
  198.5 124.6 %all-reduce.1 = (f32[128]{0:T(128)S(1)}, f32[128]{0:T(128)S(1)}) all-reduce(f32[128]{0:T(128)S(1)} %get-tuple-element.15, f32[128]{0:T(128)S(1)} %get-tuple-element.9), channel_id=1, replica_groups=mesh['prompt'=4,'vocab'=64] {'vocab'}, use_global_device_ids=true, to_apply=%region_7.8 | all-reduce | flops 256 | bytes 2048 | tf_op jit(solution)/shard_map/pmax | solution.py:30
  323.1 0.2 exponential_reduce_fusion.1
  323.3 0.2 exponential_reduce_fusion
  323.5 128.4 %all-reduce = (f32[128]{0:T(128)S(1)}, f32[128]{0:T(128)S(1)}) all-reduce(f32[128]{0:T(128)S(1)} %exponential_reduce_fusion, f32[128]{0:T(128)S(1)} %exponential_reduce_fusion.1), channel_id=1, replica_groups=mesh['prompt'=4,'vocab'=64] {'vocab'}, use_global_device_ids=true, to_apply=%region_9.10 | all-reduce | flops 256 | bytes 2048 | tf_op jit(solution)/shard_map/psum | solution.py:33
  452.0 0.5 fusion.10
  452.5 0.0 copy-done.3
  452.5 13.4 %fusion.2 = f32[128,8192]{1,0:T(8,128)} fusion(bf16[8192,1024]{1,0:T(8,128)(2,1)} %all-gather.4.cloned.1.call-done, f32[128,1024]{1,0:T(8,128)S(1)} %get-tuple-element.16, pred[128,1024]{1,0:T(8,128)(4,1)S(1)} %fusion.1, f32[128]{0:T(128)S(1)} %get-tuple-element.8, f32[128]{0:T(128)S(1)} %get-tuple-element.7, f32[128]{0:T(128)S(1)} %copy-done.3), kind=kOutput, calls=%fused_computation.8 | convolution fusion | flops 2148270080 | bytes 21628416 | tf_op jit(solution)/shard_map/dot_general | solution.py:48
  466.0 0.0 reduce-scatter.2.cloned.1.call-update
  466.0 2.4 convert_element_type.12
  468.3 0.1 dynamic_slice.9
  468.4 132.2 %reduce-scatter.2.cloned.1.call-done = f32[128,128]{1,0:T(8,128)} async-done(((f32[128,8192]{1,0:T(8,128)}), f32[128,128]{1,0:T(8,128)}) %reduce-scatter.2.cloned.1.call-update) | async-done | bytes 65552 | tf_op jit(solution)/shard_map/reduce_scatter | solution.py:54
  600.6 0.9 multiply_reduce_fusion.1
  601.5 43.7 %all-gather.1 = f32[64,1,128]{2,1,0:T(1,128)S(1)} all-gather(f32[1,1,128]{2,1,0:T(1,128)S(1)} %bitcast.8), channel_id=2, replica_groups=mesh['prompt'=4,'vocab'=64] {'vocab'}, dimensions={0}, use_global_device_ids=true | all-gather | bytes 33280 | tf_op jit(solution)/shard_map/all_gather | solution.py:57
  645.2 0.1 reduce_sum.49
  645.3 1.6 multiply_subtract_fusion
  (2 shorter events, 0.0 us)
Async XLA Ops:
  7.2 0.8 copy-start.2
  7.2 1.6 copy-start
  7.2 2.1 copy-start.1
  7.2 163.1 %all-gather.4.cloned.1.call-start = ((), (), s32[]{:S(2)}) async-start(), calls=%async_computation.1 | async-start | bytes 20971520 | tf_op jit(solution)/shard_map/all_gather | solution.py:19
  7.9 592.6 %reduce-scatter.2.cloned.1.call-start = ((), (), s32[]{:S(2)}) async-start(), calls=%async_computation.2 | async-start | bytes 4259840 | tf_op jit(solution)/shard_map/reduce_scatter | solution.py:54
  179.1 16.8 %copy-start.4 = (s32[128]{0:T(128)S(1)}, s32[128]{0:T(128)}, u32[]{:S(2)}) copy-start(s32[128]{0:T(128)} %param.10) | copy-start | bytes 1540
  179.1 273.4 %copy-start.3 = (f32[128]{0:T(128)S(1)}, f32[128]{0:T(128)}, u32[]{:S(2)}) copy-start(f32[128]{0:T(128)} %param.11) | copy-start | bytes 1540
Sparse Core Ops, SparseCore 0:
  9.8 160.4 all-gather.3
  466.1 134.4 reduce-scatter.1
